TPU v7x, 512 devices: a whole 4x4x16 slice. The times are simulated.
512 devices in a mesh: dp: 2 (over y_lo), tensor: 4 (over x), context: 64 (over z, y_hi, core).
Axes of the slice: x: 4, y: 4 (y_hi: 2, y_lo: 2; y = y_hi * 2 + y_lo), z: 16, core: 2. Of those that a mesh axis runs over, the one named last changes fastest.
Arguments:
- q_in: bfloat16 [2, 8192, 4096], P('dp', 'context', 'tensor'), may hold values from -44 to 44
- k_in: bfloat16 [2, 8192, 4096], P('dp', 'context', 'tensor'), may hold values from -6 to 6
- v_in: bfloat16 [2, 8192, 4096], P('dp', 'context', 'tensor'), may hold values from -6 to 6
- short_filt: float32 [3, 7, 4096], P(None, None, 'tensor'), may hold values from -2 to 2
- long_filt: float32 [8192, 4096], P('context', 'tensor'), may hold values from -1.1 to 1.1
- norm_gain: float32 [4096], P('tensor'), may hold values from 0.1 to 1.9
- grad_out: bfloat16 [2, 8192, 4096], P('dp', 'context', 'tensor'), may hold values from -6 to 6
Outputs:
- mixed: bfloat16 [2, 8192, 4096], P('dp', 'context', 'tensor')
- grad_inputs: bfloat16 [3, 2, 8192, 4096], P(None, 'dp', 'context', 'tensor')
- grad_long: float32 [8192, 4096], P('context', 'tensor')
- grad_short: float32 [3, 7, 4096], P(None, None, 'tensor')
All inputs are finite; a program needn't handle non-finite values.
Results may differ from a plain program's by a relative error of at most 0.00225.
Values may be sent and summed in bfloat16 or wider, within the bound.
No kernel may reach another device: no remote copies, remote signals or barrier semaphores. Data moves between devices by JAX's collectives and lax.ppermute only.
A program may use at most 128 MiB of HBM per device.

v0:
```python
import math
import jax
import jax.numpy as jnp
from jax import lax
from jax.sharding import PartitionSpec as P

D = 4096
FILT = 7
EPS = 1e-06
HIGH = lax.Precision.HIGHEST


def passed_along(shard, axis, by):
    peers = lax.axis_size(axis)
    pairs = [(i, i + by) for i in range(peers) if 0 <= i + by < peers]
    return lax.ppermute(shard, axis, pairs)


def phases(first, second, modulus):
    product = first[:, None] * second[None, :] % modulus
    return product.astype(jnp.float32) * (2.0 * math.pi / modulus)


def block_table(block_len, sign):
    index = jnp.arange(block_len, dtype=jnp.int32)
    angle = phases(index, index, block_len)
    cosine = jnp.cos(angle)
    sine = jnp.sin(angle) * sign
    return jnp.stack([jnp.stack([cosine, sine]), jnp.stack([-sine, cosine])])


def forward_rows(values, modulus):
    count, block_len, width = values.shape
    ctx_size = lax.axis_size("context")
    sub_len = block_len // ctx_size
    spread = lax.all_to_all(
        values.reshape(count, 1, block_len, width),
        "context",
        split_axis=2,
        concat_axis=1,
        tiled=True,
    )
    freq = jnp.arange(2 * ctx_size, dtype=jnp.int32)
    place = (
        jnp.arange(ctx_size, dtype=jnp.int32)[:, None] * block_len
        + lax.axis_index("context") * sub_len
        + jnp.arange(sub_len, dtype=jnp.int32)[None, :]
    )
    angle = (freq[:, None, None] * place[None] % modulus).astype(jnp.float32) * (
        2.0 * math.pi / modulus
    )
    table = jnp.stack([jnp.cos(angle), -jnp.sin(angle)])
    turned = jnp.einsum("pkcs,ncsx->npksx", table, spread, precision=HIGH)
    moved = lax.all_to_all(turned, "context", split_axis=2, concat_axis=3, tiled=True)
    return jnp.einsum("pqmb,nqjbx->npjmx", block_table(block_len, 1.0), moved, precision=HIGH)


def inverse_rows(spec, modulus):
    rows = spec.shape[2]
    block_len = spec.shape[3]
    ctx_size = lax.axis_size("context")
    index = jnp.arange(block_len, dtype=jnp.int32)
    freq = 2 * lax.axis_index("context") + jnp.arange(rows, dtype=jnp.int32)
    total = freq[:, None, None] + 2 * ctx_size * index[None, :, None]
    angle = (total * index[None, None, :] % modulus).astype(jnp.float32) * (2.0 * math.pi / modulus)
    cosine = jnp.cos(angle)
    sine = jnp.sin(angle)
    table = jnp.stack([jnp.stack([cosine, -sine]), jnp.stack([sine, cosine])])
    turned = jnp.einsum("pqjmb,nqjmx->npjbx", table, spec, precision=HIGH)
    moved = lax.all_to_all(turned, "context", split_axis=3, concat_axis=2, tiled=True)
    outer = phases(
        jnp.arange(ctx_size, dtype=jnp.int32),
        jnp.arange(2 * ctx_size, dtype=jnp.int32),
        2 * ctx_size,
    )
    real_table = jnp.stack([jnp.cos(outer), -jnp.sin(outer)])
    values = jnp.einsum("qck,nqksx->ncsx", real_table, moved, precision=HIGH) / modulus
    back = lax.all_to_all(values, "context", split_axis=1, concat_axis=2, tiled=True)
    return back.reshape(back.shape[0], back.shape[2], back.shape[3])


def shards(q_in, k_in, v_in, short_filt, long_filt, norm_gain, grad_out):
    block_len = q_in.shape[1]
    channels = q_in.shape[2]
    edge_rows = FILT - 1
    modulus = 2 * lax.axis_size("context") * block_len
    branches = jnp.stack([q_in[0], k_in[0], v_in[0]])
    before = passed_along(branches[:, block_len - edge_rows :], "context", 1)
    inputs = jnp.concatenate([before, branches], 1).astype(jnp.float32)
    shorts = jnp.zeros((3, block_len, channels), jnp.float32)
    for lag in range(FILT):
        shorts = (
            shorts
            + short_filt[:, lag][:, None, :]
            * inputs[:, edge_rows - lag : edge_rows - lag + block_len]
        )
    q_short = shorts[0]
    k_short = shorts[1]
    v_short = shorts[2]
    kv_prod = k_short * v_short
    spectra = forward_rows(jnp.stack([kv_prod, long_filt]), modulus)
    kv_real, kv_imag = (spectra[0, 0], spectra[0, 1])
    filt_real, filt_imag = (spectra[1, 0], spectra[1, 1])
    conv_spec = jnp.stack(
        [kv_real * filt_real - kv_imag * filt_imag, kv_real * filt_imag + kv_imag * filt_real]
    )[None]
    conv = inverse_rows(conv_spec, modulus)[0]
    y_out = q_short * conv
    squares = lax.psum(jnp.sum(y_out * y_out, axis=-1), "tensor")
    rms = jnp.sqrt(squares / D + EPS)[:, None]
    mixed = (y_out / rms * norm_gain).astype(jnp.bfloat16)[None]
    grad_z = grad_out[0].astype(jnp.float32) * norm_gain
    prods = lax.psum(jnp.sum(grad_z * y_out, axis=-1), "tensor")[:, None]
    grad_y = grad_z / rms - y_out * prods / (D * rms**3)
    dconv = grad_y * q_short
    grad_q = grad_y * conv
    grad_spec = forward_rows(dconv[None], modulus)[0]
    grad_real = grad_spec[0]
    grad_imag = grad_spec[1]
    dkv_spec = jnp.stack(
        [
            filt_real * grad_real + filt_imag * grad_imag,
            filt_real * grad_imag - filt_imag * grad_real,
        ]
    )
    dfilt_spec = jnp.stack(
        [kv_real * grad_real + kv_imag * grad_imag, kv_real * grad_imag - kv_imag * grad_real]
    )
    results = inverse_rows(jnp.stack([dkv_spec, dfilt_spec]), modulus)
    dkv = results[0]
    dfilt_local = results[1]
    grads = jnp.stack([grad_q, dkv * v_short, dkv * k_short])
    after = passed_along(grads[:, :edge_rows].astype(jnp.bfloat16), "context", -1).astype(
        jnp.float32
    )
    extended = jnp.concatenate([grads, after], 1)
    grad_inputs = jnp.zeros((3, block_len, channels), jnp.float32)
    for lag in range(FILT):
        grad_inputs = (
            grad_inputs + short_filt[:, lag][:, None, :] * extended[:, lag : lag + block_len]
        )
    short_local = jnp.stack(
        [
            jnp.sum(grads * inputs[:, edge_rows - lag : edge_rows - lag + block_len], axis=1)
            for lag in range(FILT)
        ],
        1,
    )
    scale = 1.0 / math.sqrt(lax.axis_size("dp") * block_len * lax.axis_size("context"))
    grad_long = lax.psum(dfilt_local, "dp") * scale
    grad_short = lax.psum(short_local, ("dp", "context")) * scale
    return (mixed, grad_inputs.astype(jnp.bfloat16)[:, None], grad_long, grad_short)


def solution(mesh):
    in_specs = (
        P("dp", "context", "tensor"),
        P("dp", "context", "tensor"),
        P("dp", "context", "tensor"),
        P(None, None, "tensor"),
        P("context", "tensor"),
        P("tensor"),
        P("dp", "context", "tensor"),
    )
    out_specs = (
        P("dp", "context", "tensor"),
        P(None, "dp", "context", "tensor"),
        P("context", "tensor"),
        P(None, None, "tensor"),
    )
    return jax.shard_map(shards, mesh=mesh, in_specs=in_specs, out_specs=out_specs, check_vma=False)
```

profile of v0, /device:TPU:1, one launch (start us, length us, event | category | flops | bytes accessed | tf_op | source)
XLA Modules:
  0.0 1352.6 jit_solution(16455876887592393104)
XLA Ops:
  11.4 6.2 collective-permute-start
  31.3 17.8 %all-to-all-start = ((f32[2,1,128,1024]{3,0,1,2:T(2,128)}), f32[2,1,128,1024]{3,0,1,2:T(2,128)S(1)}, u32[]{:S(2)}, u32[]{:S(2)}) async-start(f32[2,1,128,1024]{3,0,1,2:T(2,128)} %maximum_bitcast_fusion.4), calls=%async_computation | async-start | bytes 2097152 | tf_op jit(solution)/shard_map/all_to_all | solution.py:36
  49.5 53.7 %all-to-all-done = f32[2,1,128,1024]{3,0,1,2:T(2,128)S(1)} async-done(((f32[2,1,128,1024]{3,0,1,2:T(2,128)}), f32[2,1,128,1024]{3,0,1,2:T(2,128)S(1)}, u32[]{:S(2)}, u32[]{:S(2)}) %all-to-all-start) | async-done | bytes 1048608 | tf_op jit(solution)/shard_map/all_to_all | solution.py:36
  108.3 7.3 copy.68
  115.6 7.8 all-to-all-start.1
  124.8 184.3 %all-to-all-done.1 = f32[2,2,128,2,1024]{4,1,0,3,2:T(2,128)} async-done(((f32[2,2,128,2,1024]{4,1,0,3,2:T(2,128)}), f32[2,2,128,2,1024]{4,1,0,3,2:T(2,128)}, u32[]{:S(2)}, u32[]{:S(2)}) %all-to-all-start.1) | async-done | bytes 4194336 | tf_op jit(solution)/shard_map/all_to_all | solution.py:54
  309.1 5.4 copy.70
  314.5 8.1 fusion.4
  332.2 10.6 all-to-all-start.2
  343.0 98.5 %all-to-all-done.2 = f32[1,2,2,128,1024]{4,1,2,0,3:T(2,128)} async-done(((f32[1,2,2,128,1024]{4,1,2,0,3:T(2,128)}), f32[1,2,2,128,1024]{4,1,2,0,3:T(2,128)}, u32[]{:S(2)}, u32[]{:S(2)}) %all-to-all-start.2) | async-done | bytes 2097184 | tf_op jit(solution)/shard_map/all_to_all | solution.py:70
  454.3 7.7 all-to-all-start.3
  463.2 32.8 %all-to-all-done.3 = f32[1,64,2,1024]{3,2,0,1:T(2,128)S(1)} async-done(((f32[1,64,2,1024]{3,2,0,1:T(2,128)}), f32[1,64,2,1024]{3,2,0,1:T(2,128)S(1)}, u32[]{:S(2)}, u32[]{:S(2)}) %all-to-all-start.3) | async-done | bytes 524320 | tf_op jit(solution)/shard_map/all_to_all | solution.py:78
  499.4 9.3 all-reduce
  514.5 40.9 %all_to_all.105 = f32[1,1,128,1024]{3,0,1,2:T(1,128)} all-to-all(f32[1,1,128,1024]{3,0,1,2:T(1,128)S(1)} %fusion.48), channel_id=1, replica_groups=mesh['dp'=2,'tensor'=4,'context'=64] {'context'}, dimensions={2} | all-to-all | bytes 1048576 | tf_op jit(solution)/shard_map/all_to_all | solution.py:36
  569.1 103.5 %all_to_all.106 = f32[1,2,128,2,1024]{4,1,3,0,2:T(2,128)S(1)} all-to-all(f32[1,2,128,2,1024]{4,1,3,0,2:T(2,128)} %copy.86), channel_id=1, replica_groups=mesh['dp'=2,'tensor'=4,'context'=64] {'context'}, dimensions={2} | all-to-all | bytes 4194304 | tf_op jit(solution)/shard_map/all_to_all | solution.py:54
  689.7 7.3 copy.95
  697.1 196.5 %all_to_all.107 = f32[2,2,2,128,1024]{4,1,0,2,3:T(2,128)S(1)} all-to-all(f32[2,2,2,128,1024]{4,1,0,2,3:T(2,128)} %copy.95), channel_id=1, replica_groups=mesh['dp'=2,'tensor'=4,'context'=64] {'context'}, dimensions={3} | all-to-all | bytes 8388608 | tf_op jit(solution)/shard_map/all_to_all | solution.py:70
  893.6 5.3 copy.97
  898.8 6.0 all_to_all.95
  911.2 8.2 all-to-all-start.7
  921.1 52.3 %all-to-all-done.7 = f32[2,64,2,1024]{3,2,0,1:T(2,128)} async-done(((f32[2,64,2,1024]{3,2,0,1:T(2,128)}), f32[2,64,2,1024]{3,2,0,1:T(2,128)}, u32[]{:S(2)}, u32[]{:S(2)}) %all-to-all-start.7) | async-done | bytes 1048608 | tf_op jit(solution)/shard_map/all_to_all | solution.py:78
  977.1 7.5 fusion.41
  1009.0 289.3 %all-reduce.6.cloned.1.call-done = f32[3,7,1024]{2,0,1:T(4,128)} async-done(((f32[3,7,1024]{2,0,1:T(4,128)}), f32[3,7,1024]{2,0,1:T(4,128)}) %all-reduce.6.cloned.1.call-update) | async-done | bytes 86032 | tf_op jit(solution)/shard_map/psum | solution.py:151
  1299.9 43.4 %all-reduce.4.cloned.1.call-done = f32[128,1024]{1,0:T(8,128)} async-done(((f32[128,1024]{1,0:T(8,128)}), f32[128,1024]{1,0:T(8,128)}) %all-reduce.4.cloned.1.call-update) | async-done | bytes 524304 | tf_op jit(solution)/shard_map/psum | solution.py:150
  (151 shorter events, 127.6 us)
Async XLA Ops:
  7.2 10.5 copy-start.28
  7.2 10.7 copy-start.12
  11.4 8.9 collective-permute-start
  31.3 71.9 %all-to-all-start = ((f32[2,1,128,1024]{3,0,1,2:T(2,128)}), f32[2,1,128,1024]{3,0,1,2:T(2,128)S(1)}, u32[]{:S(2)}, u32[]{:S(2)}) async-start(f32[2,1,128,1024]{3,0,1,2:T(2,128)} %maximum_bitcast_fusion.4), calls=%async_computation | async-start | bytes 2097152 | tf_op jit(solution)/shard_map/all_to_all | solution.py:36
  49.4 58.9 %copy-start.10 = (f32[1,128,64,2]{1,2,0,3:T(8,128)}, f32[1,128,64,2]{1,2,0,3:T(8,128)S(1)}, u32[]{:S(2)}) copy-start(f32[1,128,64,2]{1,2,0,3:T(8,128)S(1)} %get-tuple-element.55) | copy-start | bytes 196612
  49.5 58.9 %copy-start.11 = (f32[1,128,64,2]{1,2,0,3:T(8,128)}, f32[1,128,64,2]{1,2,0,3:T(8,128)S(1)}, u32[]{:S(2)}) copy-start(f32[1,128,64,2]{1,2,0,3:T(8,128)S(1)} %get-tuple-element.56) | copy-start | bytes 196612
  115.6 193.4 %all-to-all-start.1 = ((f32[2,2,128,2,1024]{4,1,0,3,2:T(2,128)}), f32[2,2,128,2,1024]{4,1,0,3,2:T(2,128)}, u32[]{:S(2)}, u32[]{:S(2)}) async-start(f32[2,2,128,2,1024]{4,1,0,3,2:T(2,128)} %copy.68), calls=%async_computation.1 | async-start | bytes 8388608 | tf_op jit(solution)/shard_map/all_to_all | solution.py:54
  124.0 190.5 %copy-start.8 = (f32[1,2,128,128]{3,2,1,0:T(8,128)}, f32[1,2,128,128]{3,2,1,0:T(8,128)S(1)}, u32[]{:S(2)}) copy-start(f32[1,2,128,128]{3,2,1,0:T(8,128)S(1)} %get-tuple-element.50) | copy-start | bytes 393220
  124.0 190.5 %copy-start.9 = (f32[1,2,128,128]{3,2,1,0:T(8,128)}, f32[1,2,128,128]{3,2,1,0:T(8,128)S(1)}, u32[]{:S(2)}) copy-start(f32[1,2,128,128]{3,2,1,0:T(8,128)S(1)} %get-tuple-element.51) | copy-start | bytes 393220
  332.2 109.2 %all-to-all-start.2 = ((f32[1,2,2,128,1024]{4,1,2,0,3:T(2,128)}), f32[1,2,2,128,1024]{4,1,2,0,3:T(2,128)}, u32[]{:S(2)}, u32[]{:S(2)}) async-start(f32[1,2,2,128,1024]{4,1,2,0,3:T(2,128)} %copy.79), calls=%async_computation.2 | async-start | bytes 4194304 | tf_op jit(solution)/shard_map/all_to_all | solution.py:70
  342.9 107.1 %copy-start.13 = (f32[1,64,128]{2,1,0:T(8,128)}, f32[1,64,128]{2,1,0:T(8,128)S(1)}, u32[]{:S(2)}) copy-start(f32[1,64,128]{2,1,0:T(8,128)S(1)} %get-tuple-element.68) | copy-start | bytes 98308
  450.0 12.0 copy-start.5
  454.3 41.7 %all-to-all-start.3 = ((f32[1,64,2,1024]{3,2,0,1:T(2,128)}), f32[1,64,2,1024]{3,2,0,1:T(2,128)S(1)}, u32[]{:S(2)}, u32[]{:S(2)}) async-start(f32[1,64,2,1024]{3,2,0,1:T(2,128)} %copy.82), calls=%async_computation.3 | async-start | bytes 1048576 | tf_op jit(solution)/shard_map/all_to_all | solution.py:78
  898.8 6.0 copy-start.14
  911.2 62.2 %all-to-all-start.7 = ((f32[2,64,2,1024]{3,2,0,1:T(2,128)}), f32[2,64,2,1024]{3,2,0,1:T(2,128)}, u32[]{:S(2)}, u32[]{:S(2)}) async-start(f32[2,64,2,1024]{3,2,0,1:T(2,128)} %copy.98), calls=%async_computation.7 | async-start | bytes 2097152 | tf_op jit(solution)/shard_map/all_to_all | solution.py:78
  919.5 57.7 %copy-start.29 = (f32[1024]{0:T(1024)S(1)}, f32[1024]{0:T(1024)}, u32[]{:S(2)}) copy-start(f32[1024]{0:T(1024)} %param.12) | copy-start | bytes 12292
  919.5 57.6 %copy-start.30 = (f32[128]{0:T(128)S(1)}, f32[128]{0:T(128)}, u32[]{:S(2)}) copy-start(f32[128]{0:T(128)} %get-tuple-element.22) | copy-start | bytes 1540
  919.5 57.6 %copy-start.31 = (f32[128]{0:T(128)S(1)}, f32[128]{0:T(128)}, u32[]{:S(2)}) copy-start(f32[128]{0:T(128)} %get-tuple-element.57) | copy-start | bytes 1540
  919.5 57.6 %copy-start.32 = (f32[128]{0:T(128)S(1)}, f32[128]{0:T(128)}, u32[]{:S(2)}) copy-start(f32[128]{0:T(128)} %get-tuple-element.58) | copy-start | bytes 1540
  919.5 378.8 %all-reduce.6.cloned.1.call-start = ((), (), s32[]{:S(2)}) async-start(), calls=%async_computation.9 | async-start | bytes 229376 | tf_op jit(solution)/shard_map/psum | solution.py:151
  989.0 8.1 copy-start.7
  989.0 9.3 copy-start.6
  989.8 353.6 %all-reduce.4.cloned.1.call-start = ((), (), s32[]{:S(2)}) async-start(), calls=%async_computation.8 | async-start | bytes 1048576 | tf_op jit(solution)/shard_map/psum | solution.py:150
  992.6 8.8 collective-permute-start.1
  (18 other events, 72.9 us)
Sparse Core Ops, SparseCore 0:
  989.9 308.3 all-reduce.5
  1301.2 42.1 all-reduce.3
where the time goes:
time: 1360 us; the launch traced here: 1350 us
  waiting for transfers between devices  759 us (56%)
  blocking collectives  350 us (26%)
  local copies, waits for them, and re-layouts  81.6 us (6%)
  starting transfers between devices  63.1 us (5%)
  other arithmetic  46.6 us (3%)
  matrix products  37.2 us (3%)
  between operations  15.3 us (1%)
    psum x1, waiting for transfers between devices, shards(): grad_short = lax.psum(short_local, ('dp', 'context')) * scale  289 us
    all_to_all x1, blocking collectives, inverse_rows(): lax.all_to_all(turned, 'context', split_axis=3, concat_axis=2, tiled=True)  196 us
    all_to_all x1, waiting for transfers between devices, forward_rows(): lax.all_to_all(turned, 'context', split_axis=2, concat_axis=3, tiled=True)  184 us
    all_to_all x1, blocking collectives, forward_rows(): lax.all_to_all(turned, 'context', split_axis=2, concat_axis=3, tiled=True)  103 us
    all_to_all x1, waiting for transfers between devices, inverse_rows(): lax.all_to_all(turned, 'context', split_axis=3, concat_axis=2, tiled=True)  98.5 us
    all_to_all x2, waiting for transfers between devices, inverse_rows(): lax.all_to_all(values, 'context', split_axis=1, concat_axis=2, tiled=True)  85 us
    all_to_all x1, waiting for transfers between devices, forward_rows(): lax.all_to_all(values.reshape(count, 1, block_len, width), 'context', spl...  53.7 us
    psum x1, waiting for transfers between devices, shards(): grad_long = lax.psum(dfilt_local, 'dp') * scale  43.4 us
  transfers between devices with their start and end apart: 9, of which 9 were waited for; matrix products, arithmetic and copies ran while one was open for 1% of the time, Pallas kernels for 0%

commit v1 on v0

--- a/solution.py
+++ b/solution.py
@@ -148,7 +148,7 @@
     )
     scale = 1.0 / math.sqrt(lax.axis_size("dp") * block_len * lax.axis_size("context"))
     grad_long = lax.psum(dfilt_local, "dp") * scale
-    grad_short = lax.psum(short_local, ("dp", "context")) * scale
+    grad_short = lax.psum(lax.psum(short_local, "dp"), "context") * scale
     return (mixed, grad_inputs.astype(jnp.bfloat16)[:, None], grad_long, grad_short)
 
 

time: 1360 us -> 1520 us (1.12)
  waiting for transfers between devices: 759 us -> 922 us
    psum x1, waiting for transfers between devices: 289 us -> 462 us  [shards(): grad_short = lax.psum(lax.psum(short_local, 'dp'), 'context') * scale]
where the time goes in v1:
time: 1520 us; the launch traced here: 1510 us
  waiting for transfers between devices  922 us (61%)
  blocking collectives  350 us (23%)
  local copies, waits for them, and re-layouts  81 us (5%)
  starting transfers between devices  63 us (4%)
  other arithmetic  45.8 us (3%)
  matrix products  37.2 us (2%)
  between operations  15.3 us (1%)
    psum x1, waiting for transfers between devices, shards(): grad_short = lax.psum(lax.psum(short_local, 'dp'), 'context') * scale  462 us
    all_to_all x1, blocking collectives, inverse_rows(): lax.all_to_all(turned, 'context', split_axis=3, concat_axis=2, tiled=True)  196 us
    all_to_all x1, waiting for transfers between devices, forward_rows(): lax.all_to_all(turned, 'context', split_axis=2, concat_axis=3, tiled=True)  184 us
    all_to_all x1, blocking collectives, forward_rows(): lax.all_to_all(turned, 'context', split_axis=2, concat_axis=3, tiled=True)  103 us
    all_to_all x1, waiting for transfers between devices, inverse_rows(): lax.all_to_all(turned, 'context', split_axis=3, concat_axis=2, tiled=True)  98.3 us
    all_to_all x2, waiting for transfers between devices, inverse_rows(): lax.all_to_all(values, 'context', split_axis=1, concat_axis=2, tiled=True)  85 us
    all_to_all x1, waiting for transfers between devices, forward_rows(): lax.all_to_all(values.reshape(count, 1, block_len, width), 'context', spl...  53.7 us
    all_to_all x1, blocking collectives, forward_rows(): lax.all_to_all(values.reshape(count, 1, block_len, width), 'context', spl...  40.9 us
  transfers between devices with their start and end apart: 9, of which 9 were waited for; matrix products, arithmetic and copies ran while one was open for 1% of the time, Pallas kernels for 0%

profile of v1, /device:TPU:1, one launch (start us, length us, event | category | flops | bytes accessed | tf_op | source)
XLA Modules:
  0.0 1514.1 jit_solution(16949616875394133474)
XLA Ops:
  11.4 6.2 collective-permute-start
  31.2 17.8 %all-to-all-start = ((f32[2,1,128,1024]{3,0,1,2:T(2,128)}), f32[2,1,128,1024]{3,0,1,2:T(2,128)S(1)}, u32[]{:S(2)}, u32[]{:S(2)}) async-start(f32[2,1,128,1024]{3,0,1,2:T(2,128)} %maximum_bitcast_fusion.4), calls=%async_computation | async-start | bytes 2097152 | tf_op jit(solution)/shard_map/all_to_all | solution.py:36
  49.4 53.7 %all-to-all-done = f32[2,1,128,1024]{3,0,1,2:T(2,128)S(1)} async-done(((f32[2,1,128,1024]{3,0,1,2:T(2,128)}), f32[2,1,128,1024]{3,0,1,2:T(2,128)S(1)}, u32[]{:S(2)}, u32[]{:S(2)}) %all-to-all-start) | async-done | bytes 1048608 | tf_op jit(solution)/shard_map/all_to_all | solution.py:36
  108.3 7.3 copy.68
  115.6 7.8 all-to-all-start.1
  124.7 184.3 %all-to-all-done.1 = f32[2,2,128,2,1024]{4,1,0,3,2:T(2,128)} async-done(((f32[2,2,128,2,1024]{4,1,0,3,2:T(2,128)}), f32[2,2,128,2,1024]{4,1,0,3,2:T(2,128)}, u32[]{:S(2)}, u32[]{:S(2)}) %all-to-all-start.1) | async-done | bytes 4194336 | tf_op jit(solution)/shard_map/all_to_all | solution.py:54
  309.1 5.4 copy.70
  314.5 8.1 fusion.4
  332.2 10.6 all-to-all-start.2
  343.0 98.3 %all-to-all-done.2 = f32[1,2,2,128,1024]{4,1,2,0,3:T(2,128)} async-done(((f32[1,2,2,128,1024]{4,1,2,0,3:T(2,128)}), f32[1,2,2,128,1024]{4,1,2,0,3:T(2,128)}, u32[]{:S(2)}, u32[]{:S(2)}) %all-to-all-start.2) | async-done | bytes 2097184 | tf_op jit(solution)/shard_map/all_to_all | solution.py:70
  454.1 7.8 all-to-all-start.3
  463.2 32.8 %all-to-all-done.3 = f32[1,64,2,1024]{3,2,0,1:T(2,128)S(1)} async-done(((f32[1,64,2,1024]{3,2,0,1:T(2,128)}), f32[1,64,2,1024]{3,2,0,1:T(2,128)S(1)}, u32[]{:S(2)}, u32[]{:S(2)}) %all-to-all-start.3) | async-done | bytes 524320 | tf_op jit(solution)/shard_map/all_to_all | solution.py:78
  499.3 9.3 all-reduce
  514.5 40.9 %all_to_all.105 = f32[1,1,128,1024]{3,0,1,2:T(1,128)} all-to-all(f32[1,1,128,1024]{3,0,1,2:T(1,128)S(1)} %fusion.48), channel_id=1, replica_groups=mesh['dp'=2,'tensor'=4,'context'=64] {'context'}, dimensions={2} | all-to-all | bytes 1048576 | tf_op jit(solution)/shard_map/all_to_all | solution.py:36
  569.1 103.5 %all_to_all.106 = f32[1,2,128,2,1024]{4,1,3,0,2:T(2,128)S(1)} all-to-all(f32[1,2,128,2,1024]{4,1,3,0,2:T(2,128)} %copy.86), channel_id=1, replica_groups=mesh['dp'=2,'tensor'=4,'context'=64] {'context'}, dimensions={2} | all-to-all | bytes 4194304 | tf_op jit(solution)/shard_map/all_to_all | solution.py:54
  689.7 7.3 copy.95
  697.0 196.5 %all_to_all.107 = f32[2,2,2,128,1024]{4,1,0,2,3:T(2,128)S(1)} all-to-all(f32[2,2,2,128,1024]{4,1,0,2,3:T(2,128)} %copy.95), channel_id=1, replica_groups=mesh['dp'=2,'tensor'=4,'context'=64] {'context'}, dimensions={3} | all-to-all | bytes 8388608 | tf_op jit(solution)/shard_map/all_to_all | solution.py:70
  893.5 5.3 copy.97
  898.8 6.0 all_to_all.95
  911.2 8.2 all-to-all-start.7
  921.1 52.3 %all-to-all-done.7 = f32[2,64,2,1024]{3,2,0,1:T(2,128)} async-done(((f32[2,64,2,1024]{3,2,0,1:T(2,128)}), f32[2,64,2,1024]{3,2,0,1:T(2,128)}, u32[]{:S(2)}, u32[]{:S(2)}) %all-to-all-start.7) | async-done | bytes 1048608 | tf_op jit(solution)/shard_map/all_to_all | solution.py:78
  977.1 7.7 fusion.41
  1007.1 34.4 %all-reduce.7.cloned.1.call-done = (f32[128,1024]{1,0:T(8,128)}, f32[3,7,1024]{2,0,1:T(4,128)}) async-done(((f32[128,1024]{1,0:T(8,128)}, f32[3,7,1024]{2,0,1:T(4,128)}), (f32[128,1024]{1,0:T(8,128)}, f32[3,7,1024]{2,0,1:T(4,128)})) %all-reduce.7.cloned.1.call-update) | async-done | bytes 610320 | tf_op jit(solution)/shard_map/psum | solution.py:150
  1043.4 461.7 %all-reduce.5.cloned.1.call-done = f32[3,7,1024]{2,0,1:T(4,128)} async-done(((f32[3,7,1024]{2,0,1:T(4,128)}), f32[3,7,1024]{2,0,1:T(4,128)}) %all-reduce.5.cloned.1.call-update) | async-done | bytes 86032 | tf_op jit(solution)/shard_map/psum | solution.py:151
  (151 shorter events, 125.5 us)
Async XLA Ops:
  7.2 10.5 copy-start.28
  7.2 10.7 copy-start.12
  11.4 8.9 collective-permute-start
  31.2 71.9 %all-to-all-start = ((f32[2,1,128,1024]{3,0,1,2:T(2,128)}), f32[2,1,128,1024]{3,0,1,2:T(2,128)S(1)}, u32[]{:S(2)}, u32[]{:S(2)}) async-start(f32[2,1,128,1024]{3,0,1,2:T(2,128)} %maximum_bitcast_fusion.4), calls=%async_computation | async-start | bytes 2097152 | tf_op jit(solution)/shard_map/all_to_all | solution.py:36
  49.4 58.9 %copy-start.10 = (f32[1,128,64,2]{1,2,0,3:T(8,128)}, f32[1,128,64,2]{1,2,0,3:T(8,128)S(1)}, u32[]{:S(2)}) copy-start(f32[1,128,64,2]{1,2,0,3:T(8,128)S(1)} %get-tuple-element.57) | copy-start | bytes 196612
  49.4 58.9 %copy-start.11 = (f32[1,128,64,2]{1,2,0,3:T(8,128)}, f32[1,128,64,2]{1,2,0,3:T(8,128)S(1)}, u32[]{:S(2)}) copy-start(f32[1,128,64,2]{1,2,0,3:T(8,128)S(1)} %get-tuple-element.58) | copy-start | bytes 196612
  115.6 193.5 %all-to-all-start.1 = ((f32[2,2,128,2,1024]{4,1,0,3,2:T(2,128)}), f32[2,2,128,2,1024]{4,1,0,3,2:T(2,128)}, u32[]{:S(2)}, u32[]{:S(2)}) async-start(f32[2,2,128,2,1024]{4,1,0,3,2:T(2,128)} %copy.68), calls=%async_computation.1 | async-start | bytes 8388608 | tf_op jit(solution)/shard_map/all_to_all | solution.py:54
  124.0 190.5 %copy-start.8 = (f32[1,2,128,128]{3,2,1,0:T(8,128)}, f32[1,2,128,128]{3,2,1,0:T(8,128)S(1)}, u32[]{:S(2)}) copy-start(f32[1,2,128,128]{3,2,1,0:T(8,128)S(1)} %get-tuple-element.52) | copy-start | bytes 393220
  124.0 190.5 %copy-start.9 = (f32[1,2,128,128]{3,2,1,0:T(8,128)}, f32[1,2,128,128]{3,2,1,0:T(8,128)S(1)}, u32[]{:S(2)}) copy-start(f32[1,2,128,128]{3,2,1,0:T(8,128)S(1)} %get-tuple-element.53) | copy-start | bytes 393220
  332.2 109.0 %all-to-all-start.2 = ((f32[1,2,2,128,1024]{4,1,2,0,3:T(2,128)}), f32[1,2,2,128,1024]{4,1,2,0,3:T(2,128)}, u32[]{:S(2)}, u32[]{:S(2)}) async-start(f32[1,2,2,128,1024]{4,1,2,0,3:T(2,128)} %copy.79), calls=%async_computation.2 | async-start | bytes 4194304 | tf_op jit(solution)/shard_map/all_to_all | solution.py:70
  342.9 106.9 %copy-start.13 = (f32[1,64,128]{2,1,0:T(8,128)}, f32[1,64,128]{2,1,0:T(8,128)S(1)}, u32[]{:S(2)}) copy-start(f32[1,64,128]{2,1,0:T(8,128)S(1)} %get-tuple-element.70) | copy-start | bytes 98308
  449.8 12.1 copy-start.5
  454.1 41.8 %all-to-all-start.3 = ((f32[1,64,2,1024]{3,2,0,1:T(2,128)}), f32[1,64,2,1024]{3,2,0,1:T(2,128)S(1)}, u32[]{:S(2)}, u32[]{:S(2)}) async-start(f32[1,64,2,1024]{3,2,0,1:T(2,128)} %copy.82), calls=%async_computation.3 | async-start | bytes 1048576 | tf_op jit(solution)/shard_map/all_to_all | solution.py:78
  898.8 6.1 copy-start.14
  911.2 62.2 %all-to-all-start.7 = ((f32[2,64,2,1024]{3,2,0,1:T(2,128)}), f32[2,64,2,1024]{3,2,0,1:T(2,128)}, u32[]{:S(2)}, u32[]{:S(2)}) async-start(f32[2,64,2,1024]{3,2,0,1:T(2,128)} %copy.98), calls=%async_computation.7 | async-start | bytes 2097152 | tf_op jit(solution)/shard_map/all_to_all | solution.py:78
  919.5 57.6 %copy-start.29 = (f32[1024]{0:T(1024)S(1)}, f32[1024]{0:T(1024)}, u32[]{:S(2)}) copy-start(f32[1024]{0:T(1024)} %param.12) | copy-start | bytes 12292
  919.5 57.6 %copy-start.30 = (f32[128]{0:T(128)S(1)}, f32[128]{0:T(128)}, u32[]{:S(2)}) copy-start(f32[128]{0:T(128)} %get-tuple-element.22) | copy-start | bytes 1540
  919.5 57.6 %copy-start.31 = (f32[128]{0:T(128)S(1)}, f32[128]{0:T(128)}, u32[]{:S(2)}) copy-start(f32[128]{0:T(128)} %get-tuple-element.59) | copy-start | bytes 1540
  919.5 57.6 %copy-start.32 = (f32[128]{0:T(128)S(1)}, f32[128]{0:T(128)}, u32[]{:S(2)}) copy-start(f32[128]{0:T(128)} %get-tuple-element.60) | copy-start | bytes 1540
  919.5 122.0 %all-reduce.7.cloned.1.call-start = ((), (), s32[]{:S(2)}) async-start(), calls=%async_computation.9 | async-start | bytes 1277952 | tf_op jit(solution)/shard_map/psum | solution.py:150
  989.2 6.1 copy-start.7
  989.2 7.3 copy-start.6
  990.7 8.8 collective-permute-start.1
  997.3 507.8 %all-reduce.5.cloned.1.call-start = ((), (), s32[]{:S(2)}) async-start(), calls=%async_computation.8 | async-start | bytes 229376 | tf_op jit(solution)/shard_map/psum | solution.py:151
  (18 other events, 73.4 us)
Sparse Core Ops, SparseCore 0:
  997.4 44.0 all-reduce.6
  1044.4 460.6 all-reduce.4
